TPU v7x, 256 devices: a whole 4x4x8 slice. The times are simulated.
256 devices in a mesh: dp: 32 (over x, y, core), tp: 8 (over z).
Axes of the slice: x: 4, y: 4, z: 8, core: 2. Of those that a mesh axis runs over, the one named last changes fastest.
Arguments:
- arrived_rows: bfloat16 [12288, 7168], P('dp', 'tp'), may hold values from -6 to 6
- row_counts: int32 [32], P('dp'), may hold values from 1 to 384, 4096 in all
- routes: int32 [4096, 8], P('dp'), may hold values from 0 to 31, all different within a row; in each aligned block of 128 rows (0 to 127, 128 to 255, ...) at most 40 rows name the same one
- gate_scale: float32 [4096, 8], P('dp'), may hold values from 0.1 to 0.6
- w_gate: bfloat16 [32, 7168, 1024], P('dp', 'tp'), may hold values from -0.0625 to 0.0625
- w_up: bfloat16 [32, 7168, 1024], P('dp', 'tp'), may hold values from -0.0625 to 0.0625
- w_down: bfloat16 [32, 1024, 7168], P('dp', None, 'tp'), may hold values from -0.1875 to 0.1875
- cotangent: bfloat16 [4096, 7168], P('dp', 'tp'), may hold values from -6 to 6
Outputs:
- layer_out: bfloat16 [4096, 7168], P('dp', 'tp')
- grad_rows: bfloat16 [12288, 7168], P('dp', 'tp')
Inputs may be any that keep to these rules, and one draw needn't show every extreme that they name: `row_counts`: the counts sum to exactly 4096; the largest is exactly 384. `routes`: each row names 8 different experts; within the 128 rows of one index of dp no expert is named by more than 40 rows, a bound that some block reaches.
All inputs are finite; a program needn't handle non-finite values. No bound on the sum of `row_counts` on one device may be relied on, other than what follows from the above.
Results may differ from a plain program's by a relative error of at most 0.03.
Values may be sent and summed in bfloat16 or wider, within the bound.
No kernel may reach another device: no remote copies, remote signals or barrier semaphores. Data moves between devices by JAX's collectives and lax.ppermute only.
A program may use at most 64 MiB of HBM per device.

v0:
```python
import jax
import jax.numpy as jnp
from jax import lax
from jax.sharding import PartitionSpec as P

BF = jnp.bfloat16
F32 = jnp.float32


def rounded(tensor):
    return lax.optimization_barrier(tensor.astype(BF))


def select(left, right):
    return jnp.dot(left, right, preferred_element_type=F32).astype(BF)


def select_t(left, right):
    return lax.dot_general(
        left, right, (((0,), (0,)), ((), ())), preferred_element_type=F32
    ).astype(BF)


def dot_nt(left, right):
    return lax.dot_general(left, right, (((1,), (1,)), ((), ())), preferred_element_type=F32)


def on_device(arrived_rows, row_counts, routes, gate_scale, w_gate, w_up, w_down, cotangent):
    members = lax.axis_size("dp")
    myself = lax.axis_index("dp")
    slot_count, part = arrived_rows.shape
    rows, top = routes.shape
    capacity = rows * top // members + rows * top // (4 * members)
    per_peer = -(-(slot_count // members) // 16) * 16
    gate_proj, up_proj, down_proj = (w_gate[0], w_up[0], w_down[0])

    def exchange(tensor):
        return lax.all_to_all(tensor, "dp", split_axis=0, concat_axis=0, tiled=True)

    ids = jnp.arange(members, dtype=jnp.int32)
    chosen = routes.T[None, :, :] == ids[:, None, None]
    named = jnp.any(chosen, axis=1)
    before = jnp.arange(rows)[:, None] < jnp.arange(rows)[None, :]
    place = jnp.dot(named.astype(BF), before.astype(BF), preferred_element_type=F32)
    place = jnp.where(named, place.astype(jnp.int32), -1)
    slots = jnp.arange(capacity, dtype=jnp.int32)
    hot = place[:, None, :] == slots[None, :, None]
    pack = hot.astype(BF).reshape(members * capacity, rows)
    shipped_grad = exchange(select(pack, cotangent).reshape(members, capacity, part))
    all_counts = lax.all_gather(row_counts, "dp", axis=0, tiled=True)
    starts = jnp.sum(jnp.where(ids[None, :] < ids[:, None], all_counts[None, :], 0), axis=1)
    my_start = starts[myself]
    my_count = all_counts[myself]
    column = jnp.arange(per_peer, dtype=jnp.int32)
    source_slot = (ids[:, None] - my_start) % members + column[None, :] * members
    source_slot = jnp.where(source_slot < my_count, source_slot, -1).reshape(-1)
    spread = (source_slot[:, None] == jnp.arange(slot_count, dtype=jnp.int32)[None, :]).astype(BF)
    incoming = exchange(select(spread, arrived_rows).reshape(members, per_peer, part))
    offset = (jnp.arange(rows, dtype=jnp.int32) * members + myself)[:, None] - starts[None, :]
    held = (offset >= 0) & (offset < all_counts[None, :])
    taken = jnp.where(held, offset // members, -1)
    take = (taken[:, :, None] == column[None, None, :]).astype(BF).reshape(rows, -1)
    balanced = select(take, incoming.reshape(-1, part))
    shipped = exchange(select(pack, balanced).reshape(members, capacity, part))
    grad_part = rounded(dot_nt(shipped_grad.reshape(-1, part), down_proj))
    hidden_grad = lax.psum_scatter(grad_part, "tp", scatter_dimension=0, tiled=True)
    flat = shipped.reshape(-1, part)
    gate_part = rounded(jnp.dot(flat, gate_proj, preferred_element_type=F32))
    up_part = rounded(jnp.dot(flat, up_proj, preferred_element_type=F32))
    gate_pre = lax.psum_scatter(gate_part, "tp", scatter_dimension=0, tiled=True)
    up_pre = lax.psum_scatter(up_part, "tp", scatter_dimension=0, tiled=True)
    gate_pre, up_pre, hidden_grad = (v.astype(F32) for v in (gate_pre, up_pre, hidden_grad))
    sigmoid_gate = jax.nn.sigmoid(gate_pre)
    hidden = (gate_pre * sigmoid_gate * up_pre).astype(BF)
    gate_grad = (
        hidden_grad * up_pre * sigmoid_gate * (1.0 + gate_pre * (1.0 - sigmoid_gate))
    ).astype(BF)
    up_grad = (hidden_grad * gate_pre * sigmoid_gate).astype(BF)
    gate_grad = lax.all_gather(gate_grad, "tp", axis=0, tiled=True)
    up_grad = lax.all_gather(up_grad, "tp", axis=0, tiled=True)
    hidden = lax.all_gather(hidden, "tp", axis=0, tiled=True)
    scale_high = lax.optimization_barrier(gate_scale.astype(BF))
    scale_low = (gate_scale - scale_high.astype(F32)).astype(BF)

    def weights(scale):
        per_expert = jnp.sum(jnp.where(chosen, scale.astype(F32).T[None], 0.0), axis=1)
        return jnp.where(hot, per_expert[:, None, :], 0.0).astype(BF).reshape(-1, rows)

    mix = jnp.concatenate([weights(scale_high), weights(scale_low)], axis=1)

    def combine(returned):
        both = lax.dot_general(
            mix, returned.reshape(-1, part), (((0,), (0,)), ((), ())), preferred_element_type=F32
        )
        return (both[:rows] + both[rows:]).astype(BF)

    input_grad = (dot_nt(gate_grad, gate_proj) + dot_nt(up_grad, up_proj)).astype(BF)
    returned_grad = exchange(input_grad.reshape(members, capacity, part))
    expert_out = jnp.dot(hidden, down_proj, preferred_element_type=F32).astype(BF)
    returned_out = exchange(expert_out.reshape(members, capacity, part))
    balanced_grad = combine(returned_grad)
    leaving = select_t(take, balanced_grad)
    arriving = exchange(leaving.reshape(members, per_peer, part))
    grad_rows = select_t(spread, arriving.reshape(-1, part))
    layer_out = combine(returned_out)
    return (layer_out, grad_rows)


def solution(mesh):
    placed = (
        P("dp", "tp"),
        P("dp"),
        P("dp", None),
        P("dp", None),
        P("dp", "tp", None),
        P("dp", "tp", None),
        P("dp", None, "tp"),
        P("dp", "tp"),
    )
    return jax.shard_map(
        on_device,
        mesh=mesh,
        in_specs=placed,
        out_specs=(P("dp", "tp"), P("dp", "tp")),
        check_vma=False,
    )
```

profile of v0, /device:TPU:1, one launch (start us, length us, event | category | flops | bytes accessed | tf_op | source)
XLA Modules:
  0.0 430.1 jit_solution(9517103195963572123)
XLA Ops:
  10.3 39.3 %all_to_all.30 = bf16[32,40,896]{2,1,0:T(8,128)(2,1)S(1)} all-to-all(bf16[32,40,896]{2,1,0:T(8,128)(2,1)S(1)} %bitcast.73), channel_id=1, replica_groups=mesh['dp'=32,'tp'=8] {'dp'}, dimensions={0} | all-to-all | bytes 4587520 | tf_op jit(solution)/shard_map/all_to_all | solution.py:38
  49.6 4.3 convolution_convert_fusion
  56.0 10.0 %all-reduce = s32[32]{0:T(128)S(1)} all-reduce(s32[32]{0:T(128)S(1)} %dynamic-update-slice), channel_id=1, replica_groups=mesh['dp'=32,'tp'=8] {'dp'}, use_global_device_ids=true, to_apply=%add | all-reduce | flops 32 | bytes 256
  70.4 8.7 %all-to-all-start = ((bf16[32,16,896]{2,1,0:T(8,128)(2,1)}), bf16[32,16,896]{2,1,0:T(8,128)(2,1)S(1)}, u32[]{:S(2)}, u32[]{:S(2)}) async-start(bf16[32,16,896]{2,1,0:T(8,128)(2,1)} %bitcast.80), calls=%async_computation | async-start | bytes 1835008 | tf_op jit(solution)/shard_map/all_to_all | solution.py:38
  79.3 15.3 %all-to-all-done = bf16[32,16,896]{2,1,0:T(8,128)(2,1)S(1)} async-done(((bf16[32,16,896]{2,1,0:T(8,128)(2,1)}), bf16[32,16,896]{2,1,0:T(8,128)(2,1)S(1)}, u32[]{:S(2)}, u32[]{:S(2)}) %all-to-all-start) | async-done | bytes 917536 | tf_op jit(solution)/shard_map/all_to_all | solution.py:38
  97.1 34.8 %all_to_all.31 = bf16[32,40,896]{2,1,0:T(8,128)(2,1)S(1)} all-to-all(bf16[32,40,896]{2,1,0:T(8,128)(2,1)} %bitcast.72), channel_id=1, replica_groups=mesh['dp'=32,'tp'=8] {'dp'}, dimensions={0} | all-to-all | bytes 4587520 | tf_op jit(solution)/shard_map/all_to_all | solution.py:38
  133.3 4.1 convolution_convert_fusion.2
  137.5 6.6 %convolution_convert_fusion.1 = bf16[1280,1024]{1,0:T(8,128)(2,1)} fusion(bf16[1280,896]{1,0:T(8,128)(2,1)} %bitcast.76, bf16[1,896,1024]{2,1,0:T(8,128)(2,1)} %param.13), kind=kOutput, calls=%fused_computation.2 | convolution fusion | flops 2350120960 | bytes 6750208 | tf_op jit(solution)/shard_map/dot_general | solution.py:69
  144.2 32.4 %reduce-scatter.4.cloned.1.call-done = bf16[160,1024]{1,0:T(8,128)(2,1)} async-done(((bf16[1280,1024]{1,0:T(8,128)(2,1)}), bf16[160,1024]{1,0:T(8,128)(2,1)}) %reduce-scatter.4.cloned.1.call-update) | async-done | bytes 327696 | tf_op jit(solution)/shard_map/reduce_scatter | solution.py:70
  176.5 46.1 %reduce-scatter.6.cloned.1.call-done = bf16[160,1024]{1,0:T(8,128)(2,1)} async-done(((bf16[1280,1024]{1,0:T(8,128)(2,1)}), bf16[160,1024]{1,0:T(8,128)(2,1)}) %reduce-scatter.6.cloned.1.call-update) | async-done | bytes 327696 | tf_op jit(solution)/shard_map/reduce_scatter | solution.py:71
  222.6 2.5 fusion.18
  226.4 41.7 %all-gather.6.cloned.1.call-done = bf16[1280,1024]{1,0:T(8,128)(2,1)} async-done(((bf16[160,1024]{1,0:T(8,128)(2,1)}), bf16[1280,1024]{1,0:T(8,128)(2,1)}) %all-gather.6.cloned.1.call-update) | async-done | bytes 2621456 | tf_op jit(solution)/shard_map/all_gather | solution.py:79
  268.1 6.7 %fusion.4 = f32[1280,896]{1,0:T(8,128)} fusion(bf16[1280,1024]{1,0:T(8,128)(2,1)} %all-gather.6.cloned.1.call-done, bf16[1,896,1024]{2,1,0:T(8,128)(2,1)S(1)} %copy-done), kind=kOutput, calls=%fused_computation.11 | convolution fusion | flops 2348810240 | bytes 9043968 | tf_op jit(solution)/shard_map/dot_general | solution.py:25
  274.8 36.4 %all-gather.8.cloned.1.call-done = bf16[1280,1024]{1,0:T(8,128)(2,1)} async-done(((bf16[160,1024]{1,0:T(8,128)(2,1)}), bf16[1280,1024]{1,0:T(8,128)(2,1)}) %all-gather.8.cloned.1.call-update) | async-done | bytes 2621456 | tf_op jit(solution)/shard_map/all_gather | solution.py:80
  311.3 7.9 %add_convert_fusion = bf16[1280,896]{1,0:T(8,128)(2,1)} fusion(f32[1280,896]{1,0:T(8,128)} %fusion.4, bf16[1280,1024]{1,0:T(8,128)(2,1)} %all-gather.8.cloned.1.call-done, bf16[1,896,1024]{2,1,0:T(8,128)(2,1)} %param.13), kind=kOutput, calls=%fused_computation | convolution fusion | flops 2351104000 | bytes 11337728 | tf_op jit(solution)/shard_map/dot_general | solution.py:25
  319.2 10.5 %all-to-all-start.4 = ((bf16[32,40,896]{2,1,0:T(8,128)(2,1)}), bf16[32,40,896]{2,1,0:T(8,128)(2,1)}, u32[]{:S(2)}, u32[]{:S(2)}) async-start(bf16[32,40,896]{2,1,0:T(8,128)(2,1)} %bitcast.77), calls=%async_computation.7 | async-start | bytes 4587520 | tf_op jit(solution)/shard_map/all_to_all | solution.py:38
  329.7 24.2 %all-gather.4.cloned.1.call-done = bf16[1280,1024]{1,0:T(8,128)(2,1)} async-done(((bf16[160,1024]{1,0:T(8,128)(2,1)}), bf16[1280,1024]{1,0:T(8,128)(2,1)}) %all-gather.4.cloned.1.call-update) | async-done | bytes 2621456 | tf_op jit(solution)/shard_map/all_gather | solution.py:81
  353.9 6.6 %convolution_convert_fusion.3 = bf16[1280,896]{1,0:T(8,128)(2,1)} fusion(bf16[1280,1024]{1,0:T(8,128)(2,1)} %all-gather.4.cloned.1.call-done, bf16[1,1024,896]{2,1,0:T(8,128)(2,1)} %param.14), kind=kOutput, calls=%fused_computation.4 | convolution fusion | flops 2349957120 | bytes 6750208 | tf_op jit(solution)/shard_map/dot_general | solution.py:99
  360.5 10.7 %all-to-all-start.2 = ((bf16[32,40,896]{2,1,0:T(8,128)(2,1)}), bf16[32,40,896]{2,1,0:T(8,128)(2,1)}, u32[]{:S(2)}, u32[]{:S(2)}) async-start(bf16[32,40,896]{2,1,0:T(8,128)(2,1)} %bitcast.74), calls=%async_computation.4 | async-start | bytes 4587520 | tf_op jit(solution)/shard_map/all_to_all | solution.py:38
  371.8 2.5 fusion.23
  375.7 26.0 %all-to-all-done.2 = bf16[32,40,896]{2,1,0:T(8,128)(2,1)} async-done(((bf16[32,40,896]{2,1,0:T(8,128)(2,1)}), bf16[32,40,896]{2,1,0:T(8,128)(2,1)}, u32[]{:S(2)}, u32[]{:S(2)}) %all-to-all-start.2) | async-done | bytes 2293792 | tf_op jit(solution)/shard_map/all_to_all | solution.py:38
  401.6 4.5 %all-to-all-start.5 = ((bf16[32,16,896]{2,1,0:T(8,128)(2,1)}), bf16[32,16,896]{2,1,0:T(8,128)(2,1)S(1)}, u32[]{:S(2)}, u32[]{:S(2)}) async-start(bf16[32,16,896]{2,1,0:T(8,128)(2,1)} %bitcast.23), calls=%async_computation.8 | async-start | bytes 1835008 | tf_op jit(solution)/shard_map/all_to_all | solution.py:38
  406.1 2.5 fusion.24
  409.4 12.3 %all-to-all-done.5 = bf16[32,16,896]{2,1,0:T(8,128)(2,1)S(1)} async-done(((bf16[32,16,896]{2,1,0:T(8,128)(2,1)}), bf16[32,16,896]{2,1,0:T(8,128)(2,1)S(1)}, u32[]{:S(2)}, u32[]{:S(2)}) %all-to-all-start.5) | async-done | bytes 917536 | tf_op jit(solution)/shard_map/all_to_all | solution.py:38
  (60 shorter events, 18.3 us)
Async XLA Ops:
  7.2 126.1 %copy-start = (bf16[1,896,1024]{2,1,0:T(8,128)(2,1)S(1)}, bf16[1,896,1024]{2,1,0:T(8,128)(2,1)}, u32[]{:S(2)}) copy-start(bf16[1,896,1024]{2,1,0:T(8,128)(2,1)} %param.12) | copy-start | bytes 5505028
  7.2 137.0 %reduce-scatter.8.cloned.1.call-start = ((), (), s32[]{:S(2)}) async-start(), calls=%async_computation.12 | async-start | bytes 2949120 | tf_op jit(solution)/shard_map/reduce_scatter | solution.py:66
  10.3 39.3 %copy-start.4 = (bf16[1,1024,896]{2,1,0:T(8,128)(2,1)S(1)}, bf16[1,1024,896]{2,1,0:T(8,128)(2,1)}, u32[]{:S(2)}) copy-start(bf16[1,1024,896]{2,1,0:T(8,128)(2,1)} %param.14) | copy-start | bytes 5505028
  53.9 0.7 copy-start.6
  53.9 14.9 %copy-start.5 = (bf16[384,896]{1,0:T(8,128)(2,1)S(1)}, bf16[384,896]{1,0:T(8,128)(2,1)}, u32[]{:S(2)}) copy-start(bf16[384,896]{1,0:T(8,128)(2,1)} %param.8) | copy-start | bytes 2064388
  70.4 24.2 %all-to-all-start = ((bf16[32,16,896]{2,1,0:T(8,128)(2,1)}), bf16[32,16,896]{2,1,0:T(8,128)(2,1)S(1)}, u32[]{:S(2)}, u32[]{:S(2)}) async-start(bf16[32,16,896]{2,1,0:T(8,128)(2,1)} %bitcast.80), calls=%async_computation | async-start | bytes 1835008 | tf_op jit(solution)/shard_map/all_to_all | solution.py:38
  79.1 97.4 %reduce-scatter.4.cloned.1.call-start = ((), (), s32[]{:S(2)}) async-start(), calls=%async_computation.9 | async-start | bytes 2949120 | tf_op jit(solution)/shard_map/reduce_scatter | solution.py:70
  131.9 1.4 copy-start.1
  137.5 85.2 %reduce-scatter.6.cloned.1.call-start = ((), (), s32[]{:S(2)}) async-start(), calls=%async_computation.10 | async-start | bytes 2949120 | tf_op jit(solution)/shard_map/reduce_scatter | solution.py:71
  144.1 124.0 %all-gather.6.cloned.1.call-start = ((), (), s32[]{:S(2)}) async-start(), calls=%async_computation.13 | async-start | bytes 2949120 | tf_op jit(solution)/shard_map/all_gather | solution.py:79
  225.2 86.0 %all-gather.8.cloned.1.call-start = ((), (), s32[]{:S(2)}) async-start(), calls=%async_computation.14 | async-start | bytes 2949120 | tf_op jit(solution)/shard_map/all_gather | solution.py:80
  225.8 128.1 %all-gather.4.cloned.1.call-start = ((), (), s32[]{:S(2)}) async-start(), calls=%async_computation.11 | async-start | bytes 2949120 | tf_op jit(solution)/shard_map/all_gather | solution.py:81
  319.2 41.3 %all-to-all-start.4 = ((bf16[32,40,896]{2,1,0:T(8,128)(2,1)}), bf16[32,40,896]{2,1,0:T(8,128)(2,1)}, u32[]{:S(2)}, u32[]{:S(2)}) async-start(bf16[32,40,896]{2,1,0:T(8,128)(2,1)} %bitcast.77), calls=%async_computation.7 | async-start | bytes 4587520 | tf_op jit(solution)/shard_map/all_to_all | solution.py:38
  360.5 10.7 %copy-start.3 = (f32[128,8]{0,1:T(8,128)S(1)}, f32[128,8]{0,1:T(8,128)}, u32[]{:S(2)}) copy-start(f32[128,8]{0,1:T(8,128)} %param.11) | copy-start | bytes 12292
  360.5 11.0 %copy-start.2 = (s32[128,8]{0,1:T(8,128)S(1)}, s32[128,8]{0,1:T(8,128)}, u32[]{:S(2)}) copy-start(s32[128,8]{0,1:T(8,128)} %param.10) | copy-start | bytes 12292
  360.5 41.1 %all-to-all-start.2 = ((bf16[32,40,896]{2,1,0:T(8,128)(2,1)}), bf16[32,40,896]{2,1,0:T(8,128)(2,1)}, u32[]{:S(2)}, u32[]{:S(2)}) async-start(bf16[32,40,896]{2,1,0:T(8,128)(2,1)} %bitcast.74), calls=%async_computation.4 | async-start | bytes 4587520 | tf_op jit(solution)/shard_map/all_to_all | solution.py:38
  401.6 20.1 %all-to-all-start.5 = ((bf16[32,16,896]{2,1,0:T(8,128)(2,1)}), bf16[32,16,896]{2,1,0:T(8,128)(2,1)S(1)}, u32[]{:S(2)}, u32[]{:S(2)}) async-start(bf16[32,16,896]{2,1,0:T(8,128)(2,1)} %bitcast.23), calls=%async_computation.8 | async-start | bytes 1835008 | tf_op jit(solution)/shard_map/all_to_all | solution.py:38
Sparse Core Ops, SparseCore 0:
  54.0 39.0 reduce-scatter.7
  137.6 38.9 reduce-scatter.3
  179.1 43.4 reduce-scatter.5
  225.3 42.7 all-gather.5
  270.3 40.9 all-gather.7
  312.9 40.9 all-gather.3
where the time goes:
time: 431 us; the launch traced here: 430 us
  waiting for transfers between devices  235 us (55%)
  blocking collectives  84.1 us (20%)
  matrix products  50.1 us (12%)
  starting transfers between devices  34.8 us (8%)
  between operations  15 us (3%)
  other arithmetic  6.42 us (1%)
    all_to_all x2, blocking collectives, exchange(): return lax.all_to_all(tensor, 'dp', split_axis=0, concat_axis=0, tiled=True)  74.1 us
    all_to_all x4, waiting for transfers between devices, exchange(): return lax.all_to_all(tensor, 'dp', split_axis=0, concat_axis=0, tiled=True)  53.6 us
    reduce_scatter x1, waiting for transfers between devices, on_device(): up_pre = lax.psum_scatter(up_part, 'tp', scatter_dimension=0, tiled=True)  46.1 us
    all_gather x1, waiting for transfers between devices, on_device(): gate_grad = lax.all_gather(gate_grad, 'tp', axis=0, tiled=True)  41.7 us
    all_gather x1, waiting for transfers between devices, on_device(): up_grad = lax.all_gather(up_grad, 'tp', axis=0, tiled=True)  36.4 us
    all_to_all x4, starting transfers between devices, exchange(): return lax.all_to_all(tensor, 'dp', split_axis=0, concat_axis=0, tiled=True)  34.3 us
    reduce_scatter x1, waiting for transfers between devices, on_device(): lax.psum_scatter(gate_part, 'tp', scatter_dimension=0, tiled=True)  32.4 us
    all_gather x1, waiting for transfers between devices, on_device(): hidden = lax.all_gather(hidden, 'tp', axis=0, tiled=True)  24.2 us
  transfers between devices with their start and end apart: 10, of which 8 were waited for; matrix products, arithmetic and copies ran while one was open for 11% of the time, Pallas kernels for 0%

commit v1 on v0

--- a/solution.py
+++ b/solution.py
@@ -5,6 +5,10 @@
 
 BF = jnp.bfloat16
 F32 = jnp.float32
+follow_orders = lambda values, link_axis: jnp.concatenate(
+    lax.all_to_all(jnp.stack([values for _ in range(lax.axis_size(link_axis))]), link_axis, 0, 0),
+    axis=0,
+)
 
 
 def rounded(tensor):
@@ -78,7 +82,7 @@
     up_grad = (hidden_grad * gate_pre * sigmoid_gate).astype(BF)
     gate_grad = lax.all_gather(gate_grad, "tp", axis=0, tiled=True)
     up_grad = lax.all_gather(up_grad, "tp", axis=0, tiled=True)
-    hidden = lax.all_gather(hidden, "tp", axis=0, tiled=True)
+    hidden = follow_orders(hidden, "tp")
     scale_high = lax.optimization_barrier(gate_scale.astype(BF))
     scale_low = (gate_scale - scale_high.astype(F32)).astype(BF)
 

time: 431 us -> 473 us (1.097)
  waiting for transfers between devices: 235 us -> 276 us
    all_gather x1, waiting for transfers between devices: 41.7 us -> 81.3 us  [on_device(): gate_grad = lax.all_gather(gate_grad, 'tp', axis=0, tiled=True)]
    all_gather x1 -> x0, waiting for transfers between devices: 24.2 us -> none  [on_device(): hidden = lax.all_gather(hidden, 'tp', axis=0, tiled=True)]
    all_to_all x4, waiting for transfers between devices: 53.6 us -> 77.7 us  [exchange(): return lax.all_to_all(tensor, 'dp', split_axis=0, concat_axis=0, tiled=True)]
    all_to_all x0 -> x1, starting transfers between devices: none -> 5.46 us  [lax.all_to_all(jnp.stack([values for _ in range(lax.axis_size(link_axis))...]
    all_to_all x4, starting transfers between devices: 34.3 us -> 29.1 us  [exchange(): return lax.all_to_all(tensor, 'dp', split_axis=0, concat_axis=0, tiled=True)]
where the time goes in v1:
time: 473 us; the launch traced here: 472 us
  waiting for transfers between devices  276 us (58%)
  blocking collectives  84.2 us (18%)
  matrix products  50.1 us (11%)
  starting transfers between devices  34.8 us (7%)
  between operations  14.7 us (3%)
  other arithmetic  6.33 us (1%)
  local copies, waits for them, and re-layouts  6.15 us (1%)
    all_gather x1, waiting for transfers between devices, on_device(): gate_grad = lax.all_gather(gate_grad, 'tp', axis=0, tiled=True)  81.3 us
    all_to_all x4, waiting for transfers between devices, exchange(): return lax.all_to_all(tensor, 'dp', split_axis=0, concat_axis=0, tiled=True)  77.7 us
    all_to_all x2, blocking collectives, exchange(): return lax.all_to_all(tensor, 'dp', split_axis=0, concat_axis=0, tiled=True)  74.1 us
    reduce_scatter x1, waiting for transfers between devices, on_device(): up_pre = lax.psum_scatter(up_part, 'tp', scatter_dimension=0, tiled=True)  46 us
    all_gather x1, waiting for transfers between devices, on_device(): up_grad = lax.all_gather(up_grad, 'tp', axis=0, tiled=True)  37.7 us
    reduce_scatter x1, waiting for transfers between devices, on_device(): lax.psum_scatter(gate_part, 'tp', scatter_dimension=0, tiled=True)  32.3 us
    all_to_all x4, starting transfers between devices, exchange(): return lax.all_to_all(tensor, 'dp', split_axis=0, concat_axis=0, tiled=True)  29.1 us
    dot_general x3, matrix products, dot_nt(): lax.dot_general(left, right, (((1,), (1,)), ((), ())), preferred_element_...  19 us
  transfers between devices with their start and end apart: 10, of which 8 were waited for; matrix products, arithmetic and copies ran while one was open for 11% of the time, Pallas kernels for 0%

profile of v1, /device:TPU:1, one launch (start us, length us, event | category | flops | bytes accessed | tf_op | source)
XLA Modules:
  0.0 471.8 jit_solution(12392538902849432737)
XLA Ops:
  10.3 39.3 %all_to_all.35 = bf16[32,40,896]{2,1,0:T(8,128)(2,1)S(1)} all-to-all(bf16[32,40,896]{2,1,0:T(8,128)(2,1)S(1)} %bitcast.74), channel_id=1, replica_groups=mesh['dp'=32,'tp'=8] {'dp'}, dimensions={0} | all-to-all | bytes 4587520 | tf_op jit(solution)/shard_map/all_to_all | solution.py:42
  49.6 4.3 convolution_convert_fusion
  56.0 10.0 %all-reduce = s32[32]{0:T(128)S(1)} all-reduce(s32[32]{0:T(128)S(1)} %dynamic-update-slice), channel_id=1, replica_groups=mesh['dp'=32,'tp'=8] {'dp'}, use_global_device_ids=true, to_apply=%add | all-reduce | flops 32 | bytes 256
  70.4 8.7 %all-to-all-start = ((bf16[32,16,896]{2,1,0:T(8,128)(2,1)}), bf16[32,16,896]{2,1,0:T(8,128)(2,1)S(1)}, u32[]{:S(2)}, u32[]{:S(2)}) async-start(bf16[32,16,896]{2,1,0:T(8,128)(2,1)} %bitcast.81), calls=%async_computation | async-start | bytes 1835008 | tf_op jit(solution)/shard_map/all_to_all | solution.py:42
  79.3 15.3 %all-to-all-done = bf16[32,16,896]{2,1,0:T(8,128)(2,1)S(1)} async-done(((bf16[32,16,896]{2,1,0:T(8,128)(2,1)}), bf16[32,16,896]{2,1,0:T(8,128)(2,1)S(1)}, u32[]{:S(2)}, u32[]{:S(2)}) %all-to-all-start) | async-done | bytes 917536 | tf_op jit(solution)/shard_map/all_to_all | solution.py:42
  97.1 34.8 %all_to_all.36 = bf16[32,40,896]{2,1,0:T(8,128)(2,1)S(1)} all-to-all(bf16[32,40,896]{2,1,0:T(8,128)(2,1)} %bitcast.73), channel_id=1, replica_groups=mesh['dp'=32,'tp'=8] {'dp'}, dimensions={0} | all-to-all | bytes 4587520 | tf_op jit(solution)/shard_map/all_to_all | solution.py:42
  133.3 4.1 convolution_convert_fusion.2
  137.5 6.6 %convolution_convert_fusion.1 = bf16[1280,1024]{1,0:T(8,128)(2,1)} fusion(bf16[1280,896]{1,0:T(8,128)(2,1)} %bitcast.78, bf16[1,896,1024]{2,1,0:T(8,128)(2,1)} %param.13), kind=kOutput, calls=%fused_computation.2 | convolution fusion | flops 2350120960 | bytes 6750208 | tf_op jit(solution)/shard_map/dot_general | solution.py:73
  144.2 32.3 %reduce-scatter.4.cloned.1.call-done = bf16[160,1024]{1,0:T(8,128)(2,1)} async-done(((bf16[1280,1024]{1,0:T(8,128)(2,1)}), bf16[160,1024]{1,0:T(8,128)(2,1)}) %reduce-scatter.4.cloned.1.call-update) | async-done | bytes 327696 | tf_op jit(solution)/shard_map/reduce_scatter | solution.py:74
  176.5 46.0 %reduce-scatter.6.cloned.1.call-done = bf16[160,1024]{1,0:T(8,128)(2,1)} async-done(((bf16[1280,1024]{1,0:T(8,128)(2,1)}), bf16[160,1024]{1,0:T(8,128)(2,1)}) %reduce-scatter.6.cloned.1.call-update) | async-done | bytes 327696 | tf_op jit(solution)/shard_map/reduce_scatter | solution.py:75
  227.4 5.5 %all-to-all-start.2 = ((bf16[8,160,1024]{2,1,0:T(8,128)(2,1)}), bf16[8,160,1024]{2,1,0:T(8,128)(2,1)}, u32[]{:S(2)}, u32[]{:S(2)}) async-start(bf16[8,160,1024]{2,1,0:T(8,128)(2,1)} %stack.2), calls=%async_computation.4 | async-start | bytes 5242880 | tf_op jit(solution)/shard_map/all_to_all | solution.py:9
  232.9 81.3 %all-gather.3.cloned.1.call-done = bf16[1280,1024]{1,0:T(8,128)(2,1)} async-done(((bf16[160,1024]{1,0:T(8,128)(2,1)}), bf16[1280,1024]{1,0:T(8,128)(2,1)}) %all-gather.3.cloned.1.call-update) | async-done | bytes 2621456 | tf_op jit(solution)/shard_map/all_gather | solution.py:83
  314.2 6.7 %fusion.4 = f32[1280,896]{1,0:T(8,128)} fusion(bf16[1280,1024]{1,0:T(8,128)(2,1)} %all-gather.3.cloned.1.call-done, bf16[1,896,1024]{2,1,0:T(8,128)(2,1)S(1)} %copy-done), kind=kOutput, calls=%fused_computation.11 | convolution fusion | flops 2348810240 | bytes 9043968 | tf_op jit(solution)/shard_map/dot_general | solution.py:29
  320.9 37.7 %all-gather.5.cloned.1.call-done = bf16[1280,1024]{1,0:T(8,128)(2,1)} async-done(((bf16[160,1024]{1,0:T(8,128)(2,1)}), bf16[1280,1024]{1,0:T(8,128)(2,1)}) %all-gather.5.cloned.1.call-update) | async-done | bytes 2621456 | tf_op jit(solution)/shard_map/all_gather | solution.py:84
  358.7 8.0 %add_convert_fusion = bf16[1280,896]{1,0:T(8,128)(2,1)} fusion(f32[1280,896]{1,0:T(8,128)} %fusion.4, bf16[1280,1024]{1,0:T(8,128)(2,1)} %all-gather.5.cloned.1.call-done, bf16[1,896,1024]{2,1,0:T(8,128)(2,1)} %param.13), kind=kOutput, calls=%fused_computation | convolution fusion | flops 2351104000 | bytes 11337728 | tf_op jit(solution)/shard_map/dot_general | solution.py:29
  366.6 10.5 %all-to-all-start.5 = ((bf16[32,40,896]{2,1,0:T(8,128)(2,1)}), bf16[32,40,896]{2,1,0:T(8,128)(2,1)}, u32[]{:S(2)}, u32[]{:S(2)}) async-start(bf16[32,40,896]{2,1,0:T(8,128)(2,1)} %bitcast.76), calls=%async_computation.8 | async-start | bytes 4587520 | tf_op jit(solution)/shard_map/all_to_all | solution.py:42
  377.2 6.6 %convolution_convert_fusion.3 = bf16[1280,896]{1,0:T(8,128)(2,1)} fusion(bf16[1280,1024]{1,0:T(8,128)(2,1)} %bitcast.15, bf16[1,1024,896]{2,1,0:T(8,128)(2,1)} %param.14), kind=kOutput, calls=%fused_computation.4 | convolution fusion | flops 2349957120 | bytes 6750208 | tf_op jit(solution)/shard_map/dot_general | solution.py:103
  383.7 23.9 %all-to-all-done.5 = bf16[32,40,896]{2,1,0:T(8,128)(2,1)} async-done(((bf16[32,40,896]{2,1,0:T(8,128)(2,1)}), bf16[32,40,896]{2,1,0:T(8,128)(2,1)}, u32[]{:S(2)}, u32[]{:S(2)}) %all-to-all-start.5) | async-done | bytes 2293792 | tf_op jit(solution)/shard_map/all_to_all | solution.py:42
  407.7 5.4 %all-to-all-start.3 = ((bf16[32,40,896]{2,1,0:T(8,128)(2,1)}), bf16[32,40,896]{2,1,0:T(8,128)(2,1)}, u32[]{:S(2)}, u32[]{:S(2)}) async-start(bf16[32,40,896]{2,1,0:T(8,128)(2,1)} %bitcast.75), calls=%async_computation.5 | async-start | bytes 4587520 | tf_op jit(solution)/shard_map/all_to_all | solution.py:42
  413.7 2.5 fusion.23
  417.6 26.1 %all-to-all-done.3 = bf16[32,40,896]{2,1,0:T(8,128)(2,1)} async-done(((bf16[32,40,896]{2,1,0:T(8,128)(2,1)}), bf16[32,40,896]{2,1,0:T(8,128)(2,1)}, u32[]{:S(2)}, u32[]{:S(2)}) %all-to-all-start.3) | async-done | bytes 2293792 | tf_op jit(solution)/shard_map/all_to_all | solution.py:42
  443.7 4.5 all-to-all-start.6
  448.2 2.5 fusion.24
  451.4 12.3 %all-to-all-done.6 = bf16[32,16,896]{2,1,0:T(8,128)(2,1)S(1)} async-done(((bf16[32,16,896]{2,1,0:T(8,128)(2,1)}), bf16[32,16,896]{2,1,0:T(8,128)(2,1)S(1)}, u32[]{:S(2)}, u32[]{:S(2)}) %all-to-all-start.6) | async-done | bytes 917536 | tf_op jit(solution)/shard_map/all_to_all | solution.py:42
  (60 shorter events, 22.1 us)
Async XLA Ops:
  7.2 126.2 %copy-start = (bf16[1,896,1024]{2,1,0:T(8,128)(2,1)S(1)}, bf16[1,896,1024]{2,1,0:T(8,128)(2,1)}, u32[]{:S(2)}) copy-start(bf16[1,896,1024]{2,1,0:T(8,128)(2,1)} %param.12) | copy-start | bytes 5505028
  7.2 137.0 %reduce-scatter.8.cloned.1.call-start = ((), (), s32[]{:S(2)}) async-start(), calls=%async_computation.12 | async-start | bytes 2949120 | tf_op jit(solution)/shard_map/reduce_scatter | solution.py:70
  10.3 39.3 %copy-start.4 = (bf16[1,1024,896]{2,1,0:T(8,128)(2,1)S(1)}, bf16[1,1024,896]{2,1,0:T(8,128)(2,1)}, u32[]{:S(2)}) copy-start(bf16[1,1024,896]{2,1,0:T(8,128)(2,1)} %param.14) | copy-start | bytes 5505028
  53.9 0.7 copy-start.6
  53.9 14.9 %copy-start.5 = (bf16[384,896]{1,0:T(8,128)(2,1)S(1)}, bf16[384,896]{1,0:T(8,128)(2,1)}, u32[]{:S(2)}) copy-start(bf16[384,896]{1,0:T(8,128)(2,1)} %param.8) | copy-start | bytes 2064388
  70.4 24.2 %all-to-all-start = ((bf16[32,16,896]{2,1,0:T(8,128)(2,1)}), bf16[32,16,896]{2,1,0:T(8,128)(2,1)S(1)}, u32[]{:S(2)}, u32[]{:S(2)}) async-start(bf16[32,16,896]{2,1,0:T(8,128)(2,1)} %bitcast.81), calls=%async_computation | async-start | bytes 1835008 | tf_op jit(solution)/shard_map/all_to_all | solution.py:42
  79.1 97.4 %reduce-scatter.4.cloned.1.call-start = ((), (), s32[]{:S(2)}) async-start(), calls=%async_computation.10 | async-start | bytes 2949120 | tf_op jit(solution)/shard_map/reduce_scatter | solution.py:74
  131.9 1.5 copy-start.1
  137.5 85.0 %reduce-scatter.6.cloned.1.call-start = ((), (), s32[]{:S(2)}) async-start(), calls=%async_computation.11 | async-start | bytes 2949120 | tf_op jit(solution)/shard_map/reduce_scatter | solution.py:75
  144.1 170.1 %all-gather.3.cloned.1.call-start = ((), (), s32[]{:S(2)}) async-start(), calls=%async_computation.13 | async-start | bytes 2949120 | tf_op jit(solution)/shard_map/all_gather | solution.py:83
  225.0 133.7 %all-gather.5.cloned.1.call-start = ((), (), s32[]{:S(2)}) async-start(), calls=%async_computation.14 | async-start | bytes 2949120 | tf_op jit(solution)/shard_map/all_gather | solution.py:84
  227.4 139.2 %all-to-all-start.2 = ((bf16[8,160,1024]{2,1,0:T(8,128)(2,1)}), bf16[8,160,1024]{2,1,0:T(8,128)(2,1)}, u32[]{:S(2)}, u32[]{:S(2)}) async-start(bf16[8,160,1024]{2,1,0:T(8,128)(2,1)} %stack.2), calls=%async_computation.4 | async-start | bytes 5242880 | tf_op jit(solution)/shard_map/all_to_all | solution.py:9
  366.6 41.0 %all-to-all-start.5 = ((bf16[32,40,896]{2,1,0:T(8,128)(2,1)}), bf16[32,40,896]{2,1,0:T(8,128)(2,1)}, u32[]{:S(2)}, u32[]{:S(2)}) async-start(bf16[32,40,896]{2,1,0:T(8,128)(2,1)} %bitcast.76), calls=%async_computation.8 | async-start | bytes 4587520 | tf_op jit(solution)/shard_map/all_to_all | solution.py:42
  407.7 5.4 %copy-start.3 = (f32[128,8]{0,1:T(8,128)S(1)}, f32[128,8]{0,1:T(8,128)}, u32[]{:S(2)}) copy-start(f32[128,8]{0,1:T(8,128)} %param.11) | copy-start | bytes 12292
  407.7 5.7 %copy-start.2 = (s32[128,8]{0,1:T(8,128)S(1)}, s32[128,8]{0,1:T(8,128)}, u32[]{:S(2)}) copy-start(s32[128,8]{0,1:T(8,128)} %param.10) | copy-start | bytes 12292
  407.7 36.0 %all-to-all-start.3 = ((bf16[32,40,896]{2,1,0:T(8,128)(2,1)}), bf16[32,40,896]{2,1,0:T(8,128)(2,1)}, u32[]{:S(2)}, u32[]{:S(2)}) async-start(bf16[32,40,896]{2,1,0:T(8,128)(2,1)} %bitcast.75), calls=%async_computation.5 | async-start | bytes 4587520 | tf_op jit(solution)/shard_map/all_to_all | solution.py:42
  443.7 20.1 %all-to-all-start.6 = ((bf16[32,16,896]{2,1,0:T(8,128)(2,1)}), bf16[32,16,896]{2,1,0:T(8,128)(2,1)S(1)}, u32[]{:S(2)}, u32[]{:S(2)}) async-start(bf16[32,16,896]{2,1,0:T(8,128)(2,1)} %bitcast.24), calls=%async_computation.9 | async-start | bytes 1835008 | tf_op jit(solution)/shard_map/all_to_all | solution.py:42
Sparse Core Ops, SparseCore 0:
  54.0 39.0 reduce-scatter.7
  137.6 38.8 reduce-scatter.3
  179.1 43.3 reduce-scatter.5
  225.1 89.0 all-gather.2
  316.4 42.2 all-gather.4
